TPU v7x, 32 devices: a whole 2x2x4 slice. The times are simulated.
32 devices in a mesh: sample: 2 (over core), sx: 4 (over y, x), sy: 4 (over z).
Axes of the slice: x: 2, y: 2, z: 4, core: 2. Of those that a mesh axis runs over, the one named last changes fastest.
Arguments:
- features: bfloat16 [16, 4, 16, 32, 256], P('sx', 'sample', 'sy'), may hold values from -6 to 6
- kernel: bfloat16 [3, 3, 3, 256, 256], P(None, None, None, 'sx', 'sy'), may hold values from -0.078125 to 0.078125
- filter_bias: bfloat16 [256], P('sy'), may hold values from -3 to 3
- cotangent: bfloat16 [16, 4, 16, 32, 256], P('sx', 'sample', None, None, 'sy'), may hold values from -6 to 6
Outputs:
- output: bfloat16 [16, 4, 16, 32, 256], P('sx', 'sample', None, None, 'sy')
- input_grad: bfloat16 [16, 4, 16, 32, 256], P('sx', 'sample', 'sy')
- kernel_grad: float32 [3, 3, 3, 256, 256], P(None, None, None, 'sx', 'sy')
All inputs are finite; a program needn't handle non-finite values.
Results may differ from a plain program's by a relative error of at most 0.014.
Values may be sent and summed in bfloat16 or wider, within the bound.
A program may use at most 128 MiB of HBM per device.

v0:
```python
import jax
import jax.numpy as jnp
from jax import lax
from jax.sharding import PartitionSpec as P


def padded_2(array, sides, width):
    for axis, dim in sides:
        size, length = (lax.axis_size(axis), array.shape[dim])
        up = [(i, (i + 1) % size) for i in range(size - 1)]
        down = [(j, i) for i, j in up]
        last = lax.slice_in_dim(array, length - width, length, axis=dim)
        leading = lax.slice_in_dim(array, 0, width, axis=dim)
        before = lax.ppermute(last, axis, up)
        after = lax.ppermute(leading, axis, down)
        array = jnp.concatenate([before, array, after], axis=dim)
    return array


def slope_of(hidden):
    gate = jax.nn.sigmoid(hidden)
    return gate * (1.0 + hidden * (1.0 - gate))


def convolve(inputs, weights, pads, layout):
    return lax.conv_general_dilated(
        inputs,
        weights,
        (1, 1, 1),
        pads,
        dimension_numbers=layout,
        preferred_element_type=jnp.float32,
    )


def forward_conv(inputs, weights):
    return convolve(inputs, weights, ((0, 0), (0, 0), (0, 0)), ("DNHWC", "DHWIO", "DNHWC"))


def kernel_grad_of(window, grad_pre):
    return convolve(window, grad_pre, ((0, 0), (0, 0), (0, 0)), ("DCHWN", "DIHWO", "DHWNC"))


def local(features, kernel, filter_bias, cotangent):
    kernel_full = lax.all_gather(kernel, "sx", axis=3, tiled=True)
    edged = padded_2(features, (("sx", 0),), 1)
    band = lax.all_gather(edged, "sy", axis=2, tiled=True)
    padded = jnp.pad(band, ((0, 0), (0, 0), (1, 1), (1, 1), (0, 0)))
    hidden = forward_conv(padded, kernel_full) + filter_bias.astype(jnp.float32)
    output = jax.nn.silu(hidden).astype(jnp.bfloat16)
    grad_pre = (cotangent.astype(jnp.float32) * slope_of(hidden)).astype(jnp.bfloat16)
    grad_band = padded_2(grad_pre, (("sx", 0),), 1)
    grad_padded = jnp.pad(grad_band, ((0, 0), (0, 0), (1, 1), (1, 1), (0, 0)))
    flipped = kernel_full[::-1, ::-1, ::-1]
    partial_grad = convolve(
        grad_padded, flipped, ((0, 0), (0, 0), (0, 0)), ("DNHWC", "DHWOI", "DNHWC")
    )
    input_grad = lax.psum_scatter(
        partial_grad.astype(jnp.bfloat16), "sy", scatter_dimension=2, tiled=True
    )
    local_grad = kernel_grad_of(padded, grad_pre)
    weight_sum = lax.psum_scatter(
        local_grad.astype(jnp.bfloat16), "sx", scatter_dimension=3, tiled=True
    )
    kernel_grad = lax.psum(weight_sum, "sample").astype(jnp.float32)
    return (output, input_grad, kernel_grad)


def solution(mesh):
    return jax.shard_map(
        local,
        mesh=mesh,
        in_specs=(
            P("sx", "sample", "sy", None, None),
            P(None, None, None, "sx", "sy"),
            P("sy"),
            P("sx", "sample", None, None, "sy"),
        ),
        out_specs=(
            P("sx", "sample", None, None, "sy"),
            P("sx", "sample", "sy", None, None),
            P(None, None, None, "sx", "sy"),
        ),
        check_vma=False,
    )
```

profile of v0, /device:TPU:0, one launch (start us, length us, event | category | flops | bytes accessed | tf_op | source)
XLA Modules:
  0.0 269.2 jit_solution(10570267025638348491)
XLA Ops:
  7.2 1.6 copy.28
  9.1 4.9 %collective-permute-start = (bf16[1,2,4,32,256]{4,1,3,2,0:T(2,128)(2,1)S(1)}, bf16[1,2,4,32,256]{4,1,3,2,0:T(2,128)(2,1)S(1)}, u32[]{:S(2)}, u32[]{:S(2)}) collective-permute-start(bf16[1,2,4,32,256]{4,1,3,2,0:T(2,128)(2,1)S(1)} %get-tuple-element.13), channel_id=1, source_target_pairs={{0,4},{4,8},{8,12},{1,5},{5,9},{9,13},{2,6},{6,10},{10,14},{3,7},{... | collective-permute-start | bytes 393224 | tf_op jit(solution)/shard_map/ppermute | solution.py:14
  13.9 1.3 collective-permute-start.1
  15.2 1.4 collective-permute-done
  16.7 4.8 %collective-permute-done.1 = bf16[1,2,4,32,256]{4,1,3,2,0:T(2,128)(2,1)S(1)} collective-permute-done((bf16[1,2,4,32,256]{4,1,3,2,0:T(2,128)(2,1)S(1)}, bf16[1,2,4,32,256]{4,1,3,2,0:T(2,128)(2,1)S(1)}, u32[]{:S(2)}, u32[]{:S(2)}) %collective-permute-start.1) | collective-permute-done | bytes 131104 | tf_op jit(solution)/shard_map/ppermute | solution.py:15
  21.4 2.1 pad_maximum_fusion
  23.6 17.6 %all_gather.7 = bf16[3,3,3,256,64]{4,3,2,1,0:T(8,128)(2,1)S(1)} all-gather(bf16[3,3,3,64,64]{4,3,2,1,0:T(8,128)(2,1)S(1)} %copy-done.5), channel_id=1, replica_groups=mesh['sample'=2,'sx'=4,'sy'=4] {'sx'}, dimensions={3}, use_global_device_ids=true | all-gather | bytes 1105920 | tf_op jit(solution)/shard_map/all_gather | solution.py:45
  41.2 46.4 %all-gather.2.cloned.1.call-done = bf16[6,2,16,32,256]{4,1,3,2,0:T(2,128)(2,1)} async-done(((bf16[6,2,4,32,256]{4,1,3,2,0:T(2,128)(2,1)}), bf16[6,2,16,32,256]{4,1,3,2,0:T(2,128)(2,1)}) %all-gather.2.cloned.1.call-update) | async-done | bytes 3145744 | tf_op jit(solution)/shard_map/all_gather | solution.py:47
  87.7 4.8 %pad.4 = bf16[6,16,2,40,256]{4,2,3,1,0:T(2,128)(2,1)S(1)} pad(bf16[6,16,2,32,256]{4,2,3,1,0:T(2,128)(2,1)} %bitcast.37, bf16[]{:T(256)} %constant.6), padding=0_0x0_0x0_0x1_7x0_0 | pad | bytes 7077890 | tf_op jit(solution)/shard_map/all_gather | solution.py:47
  94.0 21.8 %add_multiply_fusion = (f32[4,16,16,5,64]{4,2,3,1,0:T(8,128)S(1)}, bf16[4,16,16,5,64]{4,2,3,1,0:T(8,128)(2,1)}) fusion(f32[64]{0:T(128)S(1)} %convert_element_type.25, pred[16,5]{0,1:T(8,128)(4,1)S(1)} %copy-done.7, bf16[3,3,3,256,64]{4,3,2,1,0:T(8,128)(2,1)S(1)} %all_gather.7, bf16[6,16,2,7,2,256]{5,3,2,4,1,0:T(8,128)(2,1)S(1)} %slice.23, ...), kind=kOutput, calls=%fused_computation.16 | convolution fusion | flops 4361224192 | bytes 8159568 | tf_op jit(solution)/shard_map/conv_general_dilated | solution.py:26
  117.6 0.8 fusion.22
  118.4 4.1 %collective-permute-start.2 = (bf16[1,2,16,32,64]{4,2,3,1,0:T(8,128)(2,1)}, bf16[1,2,16,32,64]{4,2,3,1,0:T(8,128)(2,1)}, u32[]{:S(2)}, u32[]{:S(2)}) collective-permute-start(bf16[1,2,16,32,64]{4,2,3,1,0:T(8,128)(2,1)} %get-tuple-element.11), channel_id=1, source_target_pairs={{0,4},{4,8},{8,12},{1,5},{5,9},{9,13},{2,6},{6,10},{10,14},{3,7},{... | collective-permute-start | bytes 393224 | tf_op jit(solution)/shard_map/ppermute | solution.py:14
  122.5 1.3 collective-permute-start.3
  123.8 36.4 %convolution_convert_fusion = bf16[3,3,3,256,64]{4,3,2,1,0:T(8,128)(2,1)} fusion(bf16[6,2,16,32,256]{4,1,3,2,0:T(2,128)(2,1)S(1)} %copy-done, bf16[4,2,16,32,64]{4,2,3,1,0:T(8,128)(2,1)S(1)} %fusion.15), kind=kOutput, calls=%fused_computation.24 | convolution fusion | flops 3400974336 | bytes 4554752 | tf_op jit(solution)/shard_map/conv_general_dilated | solution.py:26
  160.3 1.4 maximum_bitcast_fusion
  163.8 10.1 %select_convert_fusion = bf16[4,16,16,5,256]{4,2,3,1,0:T(8,128)(2,1)S(1)} fusion(pred[16,5]{0,1:T(8,128)(4,1)S(1)} %copy-done.8, bf16[3,3,3,256,64]{4,3,2,1,0:T(8,128)(2,1)S(1)} %copy-done.2, bf16[6,16,2,8,7,64]{5,1,4,3,2,0:T(8,128)(2,1)S(1)} %fusion.9), kind=kOutput, calls=%fused_computation.10 | convolution fusion | flops 4343726080 | bytes 4882512 | tf_op jit(solution)/shard_map/conv_general_dilated | solution.py:26
  173.8 1.0 copy.37
  174.8 17.9 %reduce-scatter.5.cloned.1.call-done = bf16[3,3,3,64,64]{4,3,2,1,0:T(8,128)(2,1)} async-done(((bf16[3,3,3,256,64]{4,3,2,1,0:T(8,128)(2,1)}), bf16[3,3,3,64,64]{4,3,2,1,0:T(8,128)(2,1)}) %reduce-scatter.5.cloned.1.call-update) | async-done | bytes 221200 | tf_op jit(solution)/shard_map/reduce_scatter | solution.py:62
  193.0 2.1 copy.38
  195.6 1.2 copy.40
  196.9 16.7 %all-reduce.2.cloned.1.call-done = bf16[3,3,3,64,64]{4,3,2,1,0:T(8,128)(2,1)} async-done(((bf16[3,3,3,64,64]{4,3,2,1,0:T(8,128)(2,1)}), bf16[3,3,3,64,64]{4,3,2,1,0:T(8,128)(2,1)}) %all-reduce.2.cloned.1.call-update) | async-done | bytes 221200 | tf_op jit(solution)/shard_map/psum | solution.py:65
  213.6 2.0 convert_element_type.31
  215.6 45.0 %reduce-scatter.3.cloned.1.call-done = bf16[4,2,4,32,256]{4,3,1,0,2:T(8,128)(2,1)} async-done(((bf16[4,2,16,32,256]{4,3,1,0,2:T(8,128)(2,1)}), bf16[4,2,4,32,256]{4,3,1,0,2:T(8,128)(2,1)}) %reduce-scatter.3.cloned.1.call-update) | async-done | bytes 524304 | tf_op jit(solution)/shard_map/reduce_scatter | solution.py:58
  260.6 1.9 copy.41
  (40 shorter events, 6.3 us)
Async XLA Ops:
  7.2 16.4 %copy-start.6 = (bf16[64]{0:T(256)(128)(2,1)S(1)}, bf16[64]{0:T(256)(128)(2,1)}, u32[]{:S(2)}) copy-start(bf16[64]{0:T(256)(128)(2,1)} %param.6) | copy-start | bytes 388
  7.2 16.4 %copy-start.5 = (bf16[3,3,3,64,64]{4,3,2,1,0:T(8,128)(2,1)S(1)}, bf16[3,3,3,64,64]{4,3,2,1,0:T(8,128)(2,1)}, u32[]{:S(2)}) copy-start(bf16[3,3,3,64,64]{4,3,2,1,0:T(8,128)(2,1)} %param.5) | copy-start | bytes 663556
  7.2 80.5 %all-gather.2.cloned.1.call-start = ((), (), s32[]{:S(2)}) async-start(), calls=%async_computation.2 | async-start | bytes 3932160 | tf_op jit(solution)/shard_map/all_gather | solution.py:47
  9.1 7.6 %collective-permute-start = (bf16[1,2,4,32,256]{4,1,3,2,0:T(2,128)(2,1)S(1)}, bf16[1,2,4,32,256]{4,1,3,2,0:T(2,128)(2,1)S(1)}, u32[]{:S(2)}, u32[]{:S(2)}) collective-permute-start(bf16[1,2,4,32,256]{4,1,3,2,0:T(2,128)(2,1)S(1)} %get-tuple-element.13), channel_id=1, source_target_pairs={{0,4},{4,8},{8,12},{1,5},{5,9},{9,13},{2,6},{6,10},{10,14},{3,7},{... | collective-permute-start | bytes 393224 | tf_op jit(solution)/shard_map/ppermute | solution.py:14
  13.9 7.5 %collective-permute-start.1 = (bf16[1,2,4,32,256]{4,1,3,2,0:T(2,128)(2,1)S(1)}, bf16[1,2,4,32,256]{4,1,3,2,0:T(2,128)(2,1)S(1)}, u32[]{:S(2)}, u32[]{:S(2)}) collective-permute-start(bf16[1,2,4,32,256]{4,1,3,2,0:T(2,128)(2,1)S(1)} %get-tuple-element.14), channel_id=1, source_target_pairs={{4,0},{8,4},{12,8},{5,1},{9,5},{13,9},{6,2},{10,6},{14,10},{7,3},{... | collective-permute-start | bytes 393224 | tf_op jit(solution)/shard_map/ppermute | solution.py:15
  23.5 169.2 %reduce-scatter.5.cloned.1.call-start = ((), (), s32[]{:S(2)}) async-start(), calls=%async_computation.4 | async-start | bytes 2211840 | tf_op jit(solution)/shard_map/reduce_scatter | solution.py:62
  41.2 52.5 %copy-start.1 = (bf16[3,3,3,256,64]{4,3,2,1,0:T(8,128)(2,1)}, bf16[3,3,3,256,64]{4,3,2,1,0:T(8,128)(2,1)S(1)}, u32[]{:S(2)}) copy-start(bf16[3,3,3,256,64]{4,3,2,1,0:T(8,128)(2,1)S(1)} %all_gather.7) | copy-start | bytes 2654212
  93.3 0.7 copy-start.7
  115.8 1.2 copy-start.4
  117.1 6.7 %copy-start = (bf16[6,2,16,32,256]{4,1,3,2,0:T(2,128)(2,1)S(1)}, bf16[6,2,16,32,256]{4,1,3,2,0:T(2,128)(2,1)}, u32[]{:S(2)}) copy-start(bf16[6,2,16,32,256]{4,1,3,2,0:T(2,128)(2,1)} %all-gather.2.cloned.1.call-done) | copy-start | bytes 9437188
  118.4 41.9 %collective-permute-start.2 = (bf16[1,2,16,32,64]{4,2,3,1,0:T(8,128)(2,1)}, bf16[1,2,16,32,64]{4,2,3,1,0:T(8,128)(2,1)}, u32[]{:S(2)}, u32[]{:S(2)}) collective-permute-start(bf16[1,2,16,32,64]{4,2,3,1,0:T(8,128)(2,1)} %get-tuple-element.11), channel_id=1, source_target_pairs={{0,4},{4,8},{8,12},{1,5},{5,9},{9,13},{2,6},{6,10},{10,14},{3,7},{... | collective-permute-start | bytes 393224 | tf_op jit(solution)/shard_map/ppermute | solution.py:14
  122.5 37.8 %collective-permute-start.3 = (bf16[1,2,16,32,64]{4,2,3,1,0:T(8,128)(2,1)}, bf16[1,2,16,32,64]{4,2,3,1,0:T(8,128)(2,1)}, u32[]{:S(2)}, u32[]{:S(2)}) collective-permute-start(bf16[1,2,16,32,64]{4,2,3,1,0:T(8,128)(2,1)} %get-tuple-element.12), channel_id=1, source_target_pairs={{4,0},{8,4},{12,8},{5,1},{9,5},{13,9},{6,2},{10,6},{14,10},{7,3},{... | collective-permute-start | bytes 393224 | tf_op jit(solution)/shard_map/ppermute | solution.py:15
  160.3 53.3 %all-reduce.2.cloned.1.call-start = ((), (), s32[]{:S(2)}) async-start(), calls=%async_computation.5 | async-start | bytes 884736 | tf_op jit(solution)/shard_map/psum | solution.py:65
  162.3 1.5 copy-start.2
  162.3 1.5 copy-start.8
  192.7 67.9 %reduce-scatter.3.cloned.1.call-start = ((), (), s32[]{:S(2)}) async-start(), calls=%async_computation.3 | async-start | bytes 2621440 | tf_op jit(solution)/shard_map/reduce_scatter | solution.py:58
  193.0 2.1 copy-start.3
Sparse Core Ops, SparseCore 0:
  23.6 63.9 all-gather.1
  160.4 32.2 reduce-scatter.4
  195.0 18.4 all-reduce.1
  215.7 44.8 reduce-scatter.2
where the time goes:
time: 272 us; the launch traced here: 269 us
  waiting for transfers between devices  132 us (49%)
  matrix products  68.3 us (25%)
  local copies, waits for them, and re-layouts  18.4 us (7%)
  blocking collectives  17.6 us (6%)
  between operations  14.2 us (5%)
  starting transfers between devices  11.7 us (4%)
  other arithmetic  6.64 us (2%)
    conv_general_dilated x3, matrix products, convolve(): lax.conv_general_dilated(inputs, weights, (1, 1, 1), pads, dimension_numb...  68.3 us
    all_gather x1, waiting for transfers between devices, local(): band = lax.all_gather(edged, 'sy', axis=2, tiled=True)  46.4 us
    reduce_scatter x1, waiting for transfers between devices, local(): lax.psum_scatter(partial_grad.astype(jnp.bfloat16), 'sy', scatter_dimensi...  45 us
    reduce_scatter x1, waiting for transfers between devices, local(): lax.psum_scatter(local_grad.astype(jnp.bfloat16), 'sx', scatter_dimension...  17.9 us
    all_gather x1, blocking collectives, local(): kernel_full = lax.all_gather(kernel, 'sx', axis=3, tiled=True)  17.6 us
    psum x1, waiting for transfers between devices, local(): kernel_grad = lax.psum(weight_sum, 'sample').astype(jnp.float32)  16.7 us
    ppermute x2, starting transfers between devices, padded_2(): before = lax.ppermute(last, axis, up)  8.97 us
    unnamed x21, local copies, waits for them, and re-layouts  6.24 us
  transfers between devices with their start and end apart: 8, of which 6 were waited for; matrix products, arithmetic and copies ran while one was open for 21% of the time, Pallas kernels for 0%

commit v1 on v0

--- a/solution.py
+++ b/solution.py
@@ -2,6 +2,11 @@
 import jax.numpy as jnp
 from jax import lax
 from jax.sharding import PartitionSpec as P
+
+
+def summed_here(x, name):
+    parts = lax.all_gather(x, name)
+    return jnp.sum(parts, axis=0)
 
 
 def padded_2(array, sides, width):
@@ -62,7 +67,7 @@
     weight_sum = lax.psum_scatter(
         local_grad.astype(jnp.bfloat16), "sx", scatter_dimension=3, tiled=True
     )
-    kernel_grad = lax.psum(weight_sum, "sample").astype(jnp.float32)
+    kernel_grad = summed_here(weight_sum, "sample").astype(jnp.float32)
     return (output, input_grad, kernel_grad)
 
 

time: 272 us -> 250 us (0.919)
  waiting for transfers between devices: 132 us -> 109 us
    psum x1 -> x0, waiting for transfers between devices: 16.7 us -> none  [local(): kernel_grad = lax.psum(weight_sum, 'sample').astype(jnp.float32)]
    reduce_scatter x1, waiting for transfers between devices: 17.9 us -> 13.9 us  [local(): lax.psum_scatter(local_grad.astype(jnp.bfloat16), 'sx', scatter_dimension...]
    reduce_scatter x1, waiting for transfers between devices: 45 us -> 42.1 us  [local(): lax.psum_scatter(partial_grad.astype(jnp.bfloat16), 'sy', scatter_dimensi...]
  transfers between devices with their start and end apart: 8 -> 7, of which waited for: 6 -> 5; matrix products, arithmetic and copies ran while one was open for 21% -> 22% of each run, Pallas kernels for 0% -> 0%
where the time goes in v1:
time: 250 us; the launch traced here: 247 us
  waiting for transfers between devices  109 us (44%)
  matrix products  68.3 us (27%)
  blocking collectives  20.3 us (8%)
  local copies, waits for them, and re-layouts  18.3 us (7%)
  between operations  14.2 us (6%)
  starting transfers between devices  11.6 us (5%)
  other arithmetic  5.86 us (2%)
    conv_general_dilated x3, matrix products, convolve(): lax.conv_general_dilated(inputs, weights, (1, 1, 1), pads, dimension_numb...  68.3 us
    all_gather x1, waiting for transfers between devices, local(): band = lax.all_gather(edged, 'sy', axis=2, tiled=True)  46.4 us
    reduce_scatter x1, waiting for transfers between devices, local(): lax.psum_scatter(partial_grad.astype(jnp.bfloat16), 'sy', scatter_dimensi...  42.1 us
    all_gather x1, blocking collectives, local(): kernel_full = lax.all_gather(kernel, 'sx', axis=3, tiled=True)  17.6 us
    reduce_scatter x1, waiting for transfers between devices, local(): lax.psum_scatter(local_grad.astype(jnp.bfloat16), 'sx', scatter_dimension...  13.9 us
    ppermute x2, starting transfers between devices, padded_2(): before = lax.ppermute(last, axis, up)  8.95 us
    unnamed x21, local copies, waits for them, and re-layouts  6.24 us
  transfers between devices with their start and end apart: 7, of which 5 were waited for; matrix products, arithmetic and copies ran while one was open for 22% of the time, Pallas kernels for 0%

profile of v1, /device:TPU:0, one launch (start us, length us, event | category | flops | bytes accessed | tf_op | source)
XLA Modules:
  0.0 247.3 jit_solution(8904170941082912715)
XLA Ops:
  7.2 1.6 copy.28
  9.1 4.9 %collective-permute-start = (bf16[1,2,4,32,256]{4,1,3,2,0:T(2,128)(2,1)S(1)}, bf16[1,2,4,32,256]{4,1,3,2,0:T(2,128)(2,1)S(1)}, u32[]{:S(2)}, u32[]{:S(2)}) collective-permute-start(bf16[1,2,4,32,256]{4,1,3,2,0:T(2,128)(2,1)S(1)} %get-tuple-element.13), channel_id=1, source_target_pairs={{0,4},{4,8},{8,12},{1,5},{5,9},{9,13},{2,6},{6,10},{10,14},{3,7},{... | collective-permute-start | bytes 393224 | tf_op jit(solution)/shard_map/ppermute | solution.py:19
  13.9 1.3 collective-permute-start.1
  15.2 1.4 collective-permute-done
  16.7 4.8 %collective-permute-done.1 = bf16[1,2,4,32,256]{4,1,3,2,0:T(2,128)(2,1)S(1)} collective-permute-done((bf16[1,2,4,32,256]{4,1,3,2,0:T(2,128)(2,1)S(1)}, bf16[1,2,4,32,256]{4,1,3,2,0:T(2,128)(2,1)S(1)}, u32[]{:S(2)}, u32[]{:S(2)}) %collective-permute-start.1) | collective-permute-done | bytes 131104 | tf_op jit(solution)/shard_map/ppermute | solution.py:20
  21.4 2.1 pad_maximum_fusion
  23.6 17.6 %all_gather.13 = bf16[3,3,3,256,64]{4,3,2,1,0:T(8,128)(2,1)S(1)} all-gather(bf16[3,3,3,64,64]{4,3,2,1,0:T(8,128)(2,1)S(1)} %copy-done.5), channel_id=1, replica_groups=mesh['sample'=2,'sx'=4,'sy'=4] {'sx'}, dimensions={3}, use_global_device_ids=true | all-gather | bytes 1105920 | tf_op jit(solution)/shard_map/all_gather | solution.py:50
  41.2 46.4 %all-gather.3.cloned.1.call-done = bf16[6,2,16,32,256]{4,1,3,2,0:T(2,128)(2,1)} async-done(((bf16[6,2,4,32,256]{4,1,3,2,0:T(2,128)(2,1)}), bf16[6,2,16,32,256]{4,1,3,2,0:T(2,128)(2,1)}) %all-gather.3.cloned.1.call-update) | async-done | bytes 3145744 | tf_op jit(solution)/shard_map/all_gather | solution.py:52
  87.7 4.8 %pad.4 = bf16[6,16,2,40,256]{4,2,3,1,0:T(2,128)(2,1)S(1)} pad(bf16[6,16,2,32,256]{4,2,3,1,0:T(2,128)(2,1)} %bitcast.39, bf16[]{:T(256)} %constant.8.clone.1), padding=0_0x0_0x0_0x1_7x0_0 | pad | bytes 7077890 | tf_op jit(solution)/shard_map/all_gather | solution.py:52
  94.0 21.8 %add_multiply_fusion = (f32[4,16,16,5,64]{4,2,3,1,0:T(8,128)S(1)}, bf16[4,16,16,5,64]{4,2,3,1,0:T(8,128)(2,1)}) fusion(f32[64]{0:T(128)S(1)} %convert_element_type.27, pred[16,5]{0,1:T(8,128)(4,1)S(1)} %copy-done.7, bf16[3,3,3,256,64]{4,3,2,1,0:T(8,128)(2,1)S(1)} %all_gather.13, bf16[6,16,2,7,2,256]{5,3,2,4,1,0:T(8,128)(2,1)S(1)} %slice.23, ...), kind=kOutput, calls=%fused_computation.16 | convolution fusion | flops 4361224192 | bytes 8159568 | tf_op jit(solution)/shard_map/conv_general_dilated | solution.py:31
  117.5 0.8 fusion.22
  118.4 4.1 %collective-permute-start.2 = (bf16[1,2,16,32,64]{4,2,3,1,0:T(8,128)(2,1)}, bf16[1,2,16,32,64]{4,2,3,1,0:T(8,128)(2,1)}, u32[]{:S(2)}, u32[]{:S(2)}) collective-permute-start(bf16[1,2,16,32,64]{4,2,3,1,0:T(8,128)(2,1)} %get-tuple-element.11), channel_id=1, source_target_pairs={{0,4},{4,8},{8,12},{1,5},{5,9},{9,13},{2,6},{6,10},{10,14},{3,7},{... | collective-permute-start | bytes 393224 | tf_op jit(solution)/shard_map/ppermute | solution.py:19
  122.4 1.3 collective-permute-start.3
  123.7 36.5 %convolution_convert_fusion = bf16[3,3,3,256,64]{4,3,2,1,0:T(8,128)(2,1)} fusion(bf16[6,2,16,32,256]{4,1,3,2,0:T(2,128)(2,1)S(1)} %copy-done, bf16[4,2,16,32,64]{4,2,3,1,0:T(8,128)(2,1)S(1)} %fusion.15), kind=kOutput, calls=%fused_computation.24 | convolution fusion | flops 3400974336 | bytes 4554752 | tf_op jit(solution)/shard_map/conv_general_dilated | solution.py:31
  160.3 1.4 maximum_bitcast_fusion
  163.7 10.1 %select_convert_fusion = bf16[4,16,16,5,256]{4,2,3,1,0:T(8,128)(2,1)S(1)} fusion(pred[16,5]{0,1:T(8,128)(4,1)S(1)} %copy-done.8, bf16[3,3,3,256,64]{4,3,2,1,0:T(8,128)(2,1)S(1)} %copy-done.2, bf16[6,16,2,8,7,64]{5,1,4,3,2,0:T(8,128)(2,1)S(1)} %fusion.9), kind=kOutput, calls=%fused_computation.10 | convolution fusion | flops 4343726080 | bytes 4882512 | tf_op jit(solution)/shard_map/conv_general_dilated | solution.py:31
  173.8 1.0 copy.37
  174.9 2.1 copy.38
  177.6 1.2 copy.40
  178.8 13.9 %reduce-scatter.5.cloned.1.call-done = bf16[3,3,3,64,64]{4,3,2,1,0:T(8,128)(2,1)} async-done(((bf16[3,3,3,256,64]{4,3,2,1,0:T(8,128)(2,1)}), bf16[3,3,3,64,64]{4,3,2,1,0:T(8,128)(2,1)}) %reduce-scatter.5.cloned.1.call-update) | async-done | bytes 221200 | tf_op jit(solution)/shard_map/reduce_scatter | solution.py:67
  192.7 2.6 %all-gather = bf16[6,3,3,64,64]{4,3,2,1,0:T(8,128)(2,1)S(1)} all-gather(bf16[3,3,3,64,64]{4,3,2,1,0:T(8,128)(2,1)} %reduce-scatter.5.cloned.1.call-done), channel_id=2, replica_groups=mesh['sample'=2,'sx'=4,'sy'=4] {'sample'}, dimensions={0}, use_global_device_ids=true | all-gather | bytes 663552 | tf_op jit(solution)/shard_map/all_gather | solution.py:8
  195.6 1.0 convert_element_type.33
  196.6 42.1 %reduce-scatter.3.cloned.1.call-done = bf16[4,2,4,32,256]{4,3,1,0,2:T(8,128)(2,1)} async-done(((bf16[4,2,16,32,256]{4,3,1,0,2:T(8,128)(2,1)}), bf16[4,2,4,32,256]{4,3,1,0,2:T(8,128)(2,1)}) %reduce-scatter.3.cloned.1.call-update) | async-done | bytes 524304 | tf_op jit(solution)/shard_map/reduce_scatter | solution.py:63
  238.6 1.9 copy.41
  (39 shorter events, 6.4 us)
Async XLA Ops:
  7.2 16.4 %copy-start.6 = (bf16[64]{0:T(256)(128)(2,1)S(1)}, bf16[64]{0:T(256)(128)(2,1)}, u32[]{:S(2)}) copy-start(bf16[64]{0:T(256)(128)(2,1)} %param.6) | copy-start | bytes 388
  7.2 16.4 %copy-start.5 = (bf16[3,3,3,64,64]{4,3,2,1,0:T(8,128)(2,1)S(1)}, bf16[3,3,3,64,64]{4,3,2,1,0:T(8,128)(2,1)}, u32[]{:S(2)}) copy-start(bf16[3,3,3,64,64]{4,3,2,1,0:T(8,128)(2,1)} %param.5) | copy-start | bytes 663556
  7.2 80.5 %all-gather.3.cloned.1.call-start = ((), (), s32[]{:S(2)}) async-start(), calls=%async_computation.2 | async-start | bytes 3932160 | tf_op jit(solution)/shard_map/all_gather | solution.py:52
  9.1 7.6 %collective-permute-start = (bf16[1,2,4,32,256]{4,1,3,2,0:T(2,128)(2,1)S(1)}, bf16[1,2,4,32,256]{4,1,3,2,0:T(2,128)(2,1)S(1)}, u32[]{:S(2)}, u32[]{:S(2)}) collective-permute-start(bf16[1,2,4,32,256]{4,1,3,2,0:T(2,128)(2,1)S(1)} %get-tuple-element.13), channel_id=1, source_target_pairs={{0,4},{4,8},{8,12},{1,5},{5,9},{9,13},{2,6},{6,10},{10,14},{3,7},{... | collective-permute-start | bytes 393224 | tf_op jit(solution)/shard_map/ppermute | solution.py:19
  13.9 7.5 %collective-permute-start.1 = (bf16[1,2,4,32,256]{4,1,3,2,0:T(2,128)(2,1)S(1)}, bf16[1,2,4,32,256]{4,1,3,2,0:T(2,128)(2,1)S(1)}, u32[]{:S(2)}, u32[]{:S(2)}) collective-permute-start(bf16[1,2,4,32,256]{4,1,3,2,0:T(2,128)(2,1)S(1)} %get-tuple-element.14), channel_id=1, source_target_pairs={{4,0},{8,4},{12,8},{5,1},{9,5},{13,9},{6,2},{10,6},{14,10},{7,3},{... | collective-permute-start | bytes 393224 | tf_op jit(solution)/shard_map/ppermute | solution.py:20
  23.5 169.2 %reduce-scatter.5.cloned.1.call-start = ((), (), s32[]{:S(2)}) async-start(), calls=%async_computation.4 | async-start | bytes 2211840 | tf_op jit(solution)/shard_map/reduce_scatter | solution.py:67
  41.2 52.5 %copy-start.1 = (bf16[3,3,3,256,64]{4,3,2,1,0:T(8,128)(2,1)}, bf16[3,3,3,256,64]{4,3,2,1,0:T(8,128)(2,1)S(1)}, u32[]{:S(2)}) copy-start(bf16[3,3,3,256,64]{4,3,2,1,0:T(8,128)(2,1)S(1)} %all_gather.13) | copy-start | bytes 2654212
  93.3 0.7 copy-start.7
  115.8 1.2 copy-start.4
  117.0 6.7 %copy-start = (bf16[6,2,16,32,256]{4,1,3,2,0:T(2,128)(2,1)S(1)}, bf16[6,2,16,32,256]{4,1,3,2,0:T(2,128)(2,1)}, u32[]{:S(2)}) copy-start(bf16[6,2,16,32,256]{4,1,3,2,0:T(2,128)(2,1)} %all-gather.3.cloned.1.call-done) | copy-start | bytes 9437188
  118.4 41.9 %collective-permute-start.2 = (bf16[1,2,16,32,64]{4,2,3,1,0:T(8,128)(2,1)}, bf16[1,2,16,32,64]{4,2,3,1,0:T(8,128)(2,1)}, u32[]{:S(2)}, u32[]{:S(2)}) collective-permute-start(bf16[1,2,16,32,64]{4,2,3,1,0:T(8,128)(2,1)} %get-tuple-element.11), channel_id=1, source_target_pairs={{0,4},{4,8},{8,12},{1,5},{5,9},{9,13},{2,6},{6,10},{10,14},{3,7},{... | collective-permute-start | bytes 393224 | tf_op jit(solution)/shard_map/ppermute | solution.py:19
  122.4 37.9 %collective-permute-start.3 = (bf16[1,2,16,32,64]{4,2,3,1,0:T(8,128)(2,1)}, bf16[1,2,16,32,64]{4,2,3,1,0:T(8,128)(2,1)}, u32[]{:S(2)}, u32[]{:S(2)}) collective-permute-start(bf16[1,2,16,32,64]{4,2,3,1,0:T(8,128)(2,1)} %get-tuple-element.12), channel_id=1, source_target_pairs={{4,0},{8,4},{12,8},{5,1},{9,5},{13,9},{6,2},{10,6},{14,10},{7,3},{... | collective-permute-start | bytes 393224 | tf_op jit(solution)/shard_map/ppermute | solution.py:20
  160.2 78.4 %reduce-scatter.3.cloned.1.call-start = ((), (), s32[]{:S(2)}) async-start(), calls=%async_computation.3 | async-start | bytes 2621440 | tf_op jit(solution)/shard_map/reduce_scatter | solution.py:63
  162.2 1.5 copy-start.2
  162.3 1.5 copy-start.8
  174.9 2.1 copy-start.3
Sparse Core Ops, SparseCore 0:
  23.6 63.9 all-gather.2
  160.4 32.2 reduce-scatter.4
  195.0 43.5 reduce-scatter.2
